TPU v7x, 32 devices: a whole 2x2x4 slice. The times are simulated.
32 devices in a mesh: groups: 2 (over y), tensor: 8 (over z, x), seq: 2 (over core).
Axes of the slice: x: 2, y: 2, z: 4, core: 2. Of those that a mesh axis runs over, the one named last changes fastest.
Arguments:
- stored_hidden: bfloat16 [4, 64, 7168], P(('groups', 'seq'), None, 'tensor'), parts along dimension 0, may hold values from -6 to 6
- w_down_kv: bfloat16 [7168, 576], P('tensor'), may hold values from -0.0625 to 0.0625
- kv_gain: bfloat16 [512], replicated, may hold values from 0.5 to 1.5
- evicted_blocks: int32 [2], P('groups'), parts along dimension 0, may hold values from 0 to 127, as said below
- query_latent: bfloat16 [64, 1536], P(('groups', 'tensor')), parts along dimension 0, may hold values from -6 to 6
- w_up_q: bfloat16 [1536, 24576], P(None, 'tensor'), may hold values from -0.15625 to 0.15625
- w_key_absorb: bfloat16 [128, 128, 512], P('tensor'), may hold values from -0.5 to 0.5
- w_value: bfloat16 [128, 512, 128], P('tensor'), may hold values from -0.25 to 0.25
- query_positions: int32 [64], P('groups'), parts along dimension 0, may hold values from 16384 to 32767
- prefix_lengths: int32 [8], P('groups'), parts along dimension 0, may hold values from 4096 to 16384, as said below
- latent_cache: bfloat16 [32768, 576], P(('groups', 'seq')), parts along dimension 0, may hold values from -500 to 500
Outputs:
- rebuilt: bfloat16 [4, 64, 576], P(('groups', 'seq'), 'tensor'), parts along dimension 0
- attended: bfloat16 [64, 16384], P('groups', 'tensor'), parts along dimension 0
There are 2 independent parts, one for each index of `groups`. A program takes and returns all parts, laid end to end along the dimension named above; an argument that names none is the same for every part. Nothing has to cross between parts.
Inputs may be any that keep to these rules, and one draw needn't show every extreme that they name: `evicted_blocks`: distinct block numbers of the cached prefix. `prefix_lengths`: one request's length is exactly 16384.
All inputs are finite; a program needn't handle non-finite values.
Results may differ from a plain program's by a relative error of at most 0.012.
The roundings to bfloat16 on the way count: a program that leaves them out, or rounds other values in their place, can miss the bound.
Values may be sent and summed in bfloat16 or wider, within the bound.
A program may use at most 64 MiB of HBM per device.

v0:
```python
import jax
import jax.numpy as jnp
from jax import lax
from jax.sharding import PartitionSpec as P

BLK = 128


neg_large = -1e30
norm_eps = 1e-06


def merged(value, axis, join):
    pieces = jax.tree.map(lambda part: lax.all_gather(part, axis), value)
    head = jax.tree.map(lambda part: part[0], pieces)
    tail = jax.tree.map(lambda part: part[1:], pieces)
    so_far, _ = lax.scan(lambda so_far, share: (join(so_far, share), None), head, tail)
    return so_far


def rotate(values, positions):
    half_dim = values.shape[-1] // 2
    freqs = 10000.0 ** (jnp.arange(half_dim, dtype=jnp.float32) * (-2.0 / values.shape[-1]))
    angle = positions.astype(jnp.float32)[..., None] * freqs
    cosine = jnp.cos(angle)
    sine = jnp.sin(angle)
    first = values[..., :half_dim]
    second = values[..., half_dim:]
    return jnp.concatenate(
        [first * cosine - second * sine, second * cosine + first * sine], axis=-1
    )


def attend(state, query_full, key_rows, key_places, usable, limit, latent_rank):
    running_max, running_sum, running_acc = state
    scores = jnp.einsum("qhc,kc->qhk", query_full, key_rows, preferred_element_type=jnp.float32)
    allowed = (usable[None, :] & (key_places[None, :] < limit[:, None]))[:, None, :]
    block_max = jnp.max(jnp.where(allowed, scores, neg_large), axis=-1)
    new_max = jnp.maximum(running_max, block_max)
    weights = jnp.where(allowed, jnp.exp(scores - new_max[..., None]), 0.0)
    factor = jnp.exp(running_max - new_max)
    running_sum = running_sum * factor + jnp.sum(weights, axis=-1)
    running_acc = running_acc * factor[..., None] + jnp.einsum(
        "qhk,kc->qhc",
        weights.astype(jnp.bfloat16),
        key_rows[:, :latent_rank],
        preferred_element_type=jnp.float32,
    )
    return (new_max, running_sum, running_acc)


def combine_parts(first_part, second_part):
    joint_max = jnp.maximum(first_part[0], second_part[0])
    scale_first = jnp.exp(first_part[0] - joint_max)
    scale_second = jnp.exp(second_part[0] - joint_max)
    joint_sum = first_part[1] * scale_first + second_part[1] * scale_second
    joint_acc = first_part[2] * scale_first[..., None] + second_part[2] * scale_second[..., None]
    return (joint_max, joint_sum, joint_acc)


def expand_values(latent_rows, value_weights):
    return jnp.einsum("qhc,hcv->qhv", latent_rows, value_weights, precision=lax.Precision.HIGHEST)


def body(
    stored_hidden,
    w_down_kv,
    kv_gain,
    evicted_blocks,
    query_latent,
    w_up_q,
    w_key_absorb,
    w_value,
    query_positions,
    prefix_lengths,
    latent_cache,
):
    tensor_count = lax.axis_size("tensor")
    tensor_index = lax.axis_index("tensor")
    prefix_index = lax.axis_index("seq")
    half_rows = stored_hidden.shape[1]
    local_rows = half_rows // tensor_count
    latent_rank = kv_gain.shape[0]
    heads_dev = w_key_absorb.shape[0]
    nope_dim = w_key_absorb.shape[1]
    head_qk = w_up_q.shape[1] // heads_dev
    query_total = query_positions.shape[0]
    requests = prefix_lengths.shape[0]
    cache_rows = latent_cache.shape[0]
    block_ids = jnp.arange(evicted_blocks.shape[0], dtype=jnp.int32)
    value_weights = w_value.astype(jnp.float32)

    def evicted_position(flat_rows):
        owner_block = jnp.where(
            (flat_rows // BLK)[:, None] == block_ids[None, :], evicted_blocks[None, :], 0
        )
        return jnp.sum(owner_block, axis=1) * BLK + flat_rows % BLK

    query_scale = float(head_qk) ** (-0.5)
    latent_piece = lax.all_gather(query_latent, "tensor", axis=0, tiled=True)
    piece_rows = latent_piece.shape[0]
    projected = jnp.dot(latent_piece, w_up_q, preferred_element_type=jnp.float32).reshape(
        piece_rows, heads_dev, head_qk
    )
    query_nope = projected[..., :nope_dim].astype(jnp.bfloat16)
    absorbed = jnp.einsum(
        "rhn,hnc->rhc", query_nope, w_key_absorb, preferred_element_type=jnp.float32
    )
    rotated = rotate(projected[..., nope_dim:], query_positions[:, None])
    query_full = (jnp.concatenate([absorbed, rotated], axis=-1) * query_scale).astype(jnp.bfloat16)
    request_of = jnp.arange(query_total, dtype=jnp.int32) // (query_total // requests)
    request_ids = jnp.arange(requests, dtype=jnp.int32)
    limit = jnp.sum(
        jnp.where(request_of[:, None] == request_ids[None, :], prefix_lengths[None, :], 0), axis=1
    )
    block_keys = min(1024, cache_rows)
    initial = (
        jnp.full((query_total, heads_dev), neg_large, jnp.float32),
        jnp.zeros((query_total, heads_dev), jnp.float32),
        jnp.zeros((query_total, heads_dev, latent_rank), jnp.float32),
    )

    def resident_step(step_index, state):
        offset = step_index * block_keys
        key_rows = lax.dynamic_slice_in_dim(latent_cache, offset, block_keys, 0)
        key_places = prefix_index * cache_rows + offset + jnp.arange(block_keys, dtype=jnp.int32)
        stale = jnp.any((key_places // BLK)[:, None] == evicted_blocks[None, :], axis=1)
        return attend(
            state, query_full, key_rows, key_places, jnp.logical_not(stale), limit, latent_rank
        )

    state = lax.fori_loop(0, cache_rows // block_keys, resident_step, initial)
    hidden_rows = stored_hidden[0]
    half_first = prefix_index * half_rows
    summed = lax.psum(jnp.dot(hidden_rows, w_down_kv, preferred_element_type=jnp.float32), "tensor")
    latent = summed[:, :latent_rank]
    mean_square = jnp.mean(latent * latent, axis=-1, keepdims=True)
    normed = latent / jnp.sqrt(mean_square + norm_eps) * kv_gain.astype(jnp.float32)
    flat_rows = half_first + jnp.arange(summed.shape[0], dtype=jnp.int32)
    rotated = rotate(summed[:, latent_rank:], evicted_position(flat_rows))
    all_rebuilt = jnp.concatenate([normed, rotated], axis=-1).astype(jnp.bfloat16)
    all_places = evicted_position(half_first + jnp.arange(half_rows, dtype=jnp.int32))
    everyone = jnp.ones((half_rows,), dtype=jnp.bool_)
    state = attend(state, query_full, all_rebuilt, all_places, everyone, limit, latent_rank)
    rebuilt_local = lax.dynamic_slice_in_dim(all_rebuilt, tensor_index * local_rows, local_rows, 0)
    whole_max, whole_sum, whole_acc = merged((state[0], state[1], state[2]), "seq", combine_parts)
    latent_out = whole_acc / whole_sum[..., None]
    expanded = expand_values(latent_out, value_weights).astype(jnp.bfloat16)
    attended = expanded.reshape(query_total, -1)
    return (rebuilt_local[None], attended)


def solution(mesh):
    placed = (
        P(("groups", "seq"), None, "tensor"),
        P("tensor", None),
        P(),
        P("groups"),
        P(("groups", "tensor"), None),
        P(None, "tensor"),
        P("tensor", None, None),
        P("tensor", None, None),
        P("groups"),
        P("groups"),
        P(("groups", "seq"), None),
    )
    return jax.shard_map(
        body,
        mesh=mesh,
        in_specs=placed,
        out_specs=(P(("groups", "seq"), "tensor", None), P("groups", "tensor")),
        check_vma=False,
    )
```

profile of v0, /device:TPU:0, one launch (start us, length us, event | category | flops | bytes accessed | tf_op | source)
XLA Modules:
  0.0 163.4 jit_solution(16818871855866706124)
XLA Ops:
  7.2 2.5 %fusion.28 = f32[64,576]{0,1:T(8,128)} fusion(bf16[896,576]{0,1:T(8,128)(2,1)} %param.14, bf16[1,64,896]{2,1,0:T(8,128)(2,1)} %param.13), kind=kOutput, calls=%fused_computation.58 | convolution fusion | flops 66060288 | bytes 1294336 | tf_op jit(solution)/shard_map/dot_general | solution.py:135
  9.9 32.7 %all-gather.3 = bf16[8,4,1536]{2,1,0:T(4,128)(2,1)S(1)} all-gather(bf16[1,4,1536]{2,1,0:T(4,128)(2,1)} %bitcast.97), channel_id=1, replica_groups=mesh['groups'=2,'tensor'=8,'seq'=2] {'tensor'}, dimensions={0}, use_global_device_ids=true | all-gather | bytes 110592 | tf_op jit(solution)/shard_map/all_gather | solution.py:100
  42.6 5.4 %fusion.50 = f32[32,3072]{1,0:T(8,128)S(1)} fusion(bf16[32,1536]{1,0:T(8,128)(2,1)S(1)} %reshape.341, bf16[1536,3072]{1,0:T(8,128)(2,1)} %param.18), kind=kOutput, calls=%fused_computation.105 | convolution fusion | flops 301989888 | bytes 9928704 | tf_op jit(solution)/shard_map/dot_general | solution.py:102
  48.1 0.2 reshape.323
  48.3 0.1 fusion.49
  49.3 0.1 multiply_cosine_fusion
  49.4 0.4 convolution_bitcast_fusion
  49.8 0.2 multiply_subtract_fusion
  50.0 1.1 fusion.17
  51.1 81.2 %while.26 = (s32[]{:T(128)}, f32[32,16]{0,1:T(8,128)S(1)}, f32[32,16]{0,1:T(8,128)S(1)}, f32[32,16,512]{2,1,0:T(8,128)}, s32[]{:T(128)}, /*index=5*/s32[1]{0:T(1...) while((s32[]{:T(128)}, f32[32,16]{0,1:T(8,128)S(1)}, ...), condition=%wide.region_6.7_spmd.clone, body=%wide.region_3.6_spmd.clone.sunk | while | flops 1144870400 | bytes 11415903 | solution.py:132
  51.1 0.7 fusion.66
  51.7 0.1 compare_and_fusion.2
  51.8 3.8 %fusion.67 = (f32[32,16]{0,1:T(8,128)S(1)}, f32[1024,32,16]{0,1,2:T(8,128)}) fusion(pred[32,1024]{1,0:T(8,128)(4,1)S(1)} %compare_and_fusion.2, bf16[32,16,576]{2,0,1:T(8,128)(2,1)} %get-tuple-element.425, bf16[8192,576]{0,1:T(8,128)(2,1)} %get-tuple-element.424, s32[]{:T(128)S(6)} %select_n.175), kind=kOutput, calls=%fused_computation.2.clone.1 | convolution fusion | flops 605027840 | bytes 3966980 | tf_op jit(solution)/shard_map/while/body/eval_jaxpr/qhc,kc->qhk/dot_general | solution.py:36
  55.6 2.1 %fusion.68 = (bf16[32,16,1024]{2,0,1:T(8,128)(2,1)S(1)}, f32[32,16]{0,1:T(8,128)S(1)}) fusion(f32[1024,32,16]{0,1,2:T(8,128)} %get-tuple-element.386, f32[32,16]{0,1:T(8,128)S(1)} %select_maximum_fusion.2, pred[32,1024]{1,0:T(8,128)(4,1)S(1)} %compare_and_fusion.2), kind=kLoop, calls=%fused_computation.5.clone.1 | loop fusion | flops 2096640 | bytes 3182592 | tf_op jit(solution)/shard_map/while/body/eval_jaxpr/convert_element_type | solution.py:45
  57.9 3.1 %convolution_add_fusion.3 = f32[32,16,512]{2,1,0:T(8,128)} fusion(bf16[8192,576]{0,1:T(8,128)(2,1)} %get-tuple-element.424, s32[]{:T(128)S(6)} %select_n.175, bf16[32,16,1024]{2,0,1:T(8,128)(2,1)S(1)} %get-tuple-element.389, f32[32,16,512]{2,1,0:T(8,128)} %get-tuple-element.407, f32[32,16]{1,0:T(8,128)S(1)} %copy.157, pred[]{:T(512)S(6)} %compare.50), kind=kOutput, calls=%fused_computation.7.clone.1 | convolution fusion | flops 537657344 | bytes 4196357 | tf_op jit(solution)/shard_map/while/body/eval_jaxpr/qhk,kc->qhc/dot_general | solution.py:43
  61.0 0.7 fusion.66
  61.6 0.1 compare_and_fusion.2
  61.7 3.8 %fusion.67 = (f32[32,16]{0,1:T(8,128)S(1)}, f32[1024,32,16]{0,1,2:T(8,128)}) fusion(pred[32,1024]{1,0:T(8,128)(4,1)S(1)} %compare_and_fusion.2, bf16[32,16,576]{2,0,1:T(8,128)(2,1)} %get-tuple-element.425, bf16[8192,576]{0,1:T(8,128)(2,1)} %get-tuple-element.424, s32[]{:T(128)S(6)} %select_n.175), kind=kOutput, calls=%fused_computation.2.clone.1 | convolution fusion | flops 605027840 | bytes 3966980 | tf_op jit(solution)/shard_map/while/body/eval_jaxpr/qhc,kc->qhk/dot_general | solution.py:36
  65.5 2.1 %fusion.68 = (bf16[32,16,1024]{2,0,1:T(8,128)(2,1)S(1)}, f32[32,16]{0,1:T(8,128)S(1)}) fusion(f32[1024,32,16]{0,1,2:T(8,128)} %get-tuple-element.386, f32[32,16]{0,1:T(8,128)S(1)} %select_maximum_fusion.2, pred[32,1024]{1,0:T(8,128)(4,1)S(1)} %compare_and_fusion.2), kind=kLoop, calls=%fused_computation.5.clone.1 | loop fusion | flops 2096640 | bytes 3182592 | tf_op jit(solution)/shard_map/while/body/eval_jaxpr/convert_element_type | solution.py:45
  67.7 3.4 %convolution_add_fusion.3 = f32[32,16,512]{2,1,0:T(8,128)} fusion(bf16[8192,576]{0,1:T(8,128)(2,1)} %get-tuple-element.424, s32[]{:T(128)S(6)} %select_n.175, bf16[32,16,1024]{2,0,1:T(8,128)(2,1)S(1)} %get-tuple-element.389, f32[32,16,512]{2,1,0:T(8,128)} %get-tuple-element.407, f32[32,16]{1,0:T(8,128)S(1)} %copy.157, pred[]{:T(512)S(6)} %compare.50), kind=kOutput, calls=%fused_computation.7.clone.1 | convolution fusion | flops 537657344 | bytes 4196357 | tf_op jit(solution)/shard_map/while/body/eval_jaxpr/qhk,kc->qhc/dot_general | solution.py:43
  71.1 0.7 fusion.66
  71.8 0.1 compare_and_fusion.2
  71.9 3.8 %fusion.67 = (f32[32,16]{0,1:T(8,128)S(1)}, f32[1024,32,16]{0,1,2:T(8,128)}) fusion(pred[32,1024]{1,0:T(8,128)(4,1)S(1)} %compare_and_fusion.2, bf16[32,16,576]{2,0,1:T(8,128)(2,1)} %get-tuple-element.425, bf16[8192,576]{0,1:T(8,128)(2,1)} %get-tuple-element.424, s32[]{:T(128)S(6)} %select_n.175), kind=kOutput, calls=%fused_computation.2.clone.1 | convolution fusion | flops 605027840 | bytes 3966980 | tf_op jit(solution)/shard_map/while/body/eval_jaxpr/qhc,kc->qhk/dot_general | solution.py:36
  75.7 2.1 %fusion.68 = (bf16[32,16,1024]{2,0,1:T(8,128)(2,1)S(1)}, f32[32,16]{0,1:T(8,128)S(1)}) fusion(f32[1024,32,16]{0,1,2:T(8,128)} %get-tuple-element.386, f32[32,16]{0,1:T(8,128)S(1)} %select_maximum_fusion.2, pred[32,1024]{1,0:T(8,128)(4,1)S(1)} %compare_and_fusion.2), kind=kLoop, calls=%fused_computation.5.clone.1 | loop fusion | flops 2096640 | bytes 3182592 | tf_op jit(solution)/shard_map/while/body/eval_jaxpr/convert_element_type | solution.py:45
  78.0 3.4 %convolution_add_fusion.3 = f32[32,16,512]{2,1,0:T(8,128)} fusion(bf16[8192,576]{0,1:T(8,128)(2,1)} %get-tuple-element.424, s32[]{:T(128)S(6)} %select_n.175, bf16[32,16,1024]{2,0,1:T(8,128)(2,1)S(1)} %get-tuple-element.389, f32[32,16,512]{2,1,0:T(8,128)} %get-tuple-element.407, f32[32,16]{1,0:T(8,128)S(1)} %copy.157, pred[]{:T(512)S(6)} %compare.50), kind=kOutput, calls=%fused_computation.7.clone.1 | convolution fusion | flops 537657344 | bytes 4196357 | tf_op jit(solution)/shard_map/while/body/eval_jaxpr/qhk,kc->qhc/dot_general | solution.py:43
  81.4 0.7 fusion.66
  82.0 0.1 compare_and_fusion.2
  82.1 3.8 %fusion.67 = (f32[32,16]{0,1:T(8,128)S(1)}, f32[1024,32,16]{0,1,2:T(8,128)}) fusion(pred[32,1024]{1,0:T(8,128)(4,1)S(1)} %compare_and_fusion.2, bf16[32,16,576]{2,0,1:T(8,128)(2,1)} %get-tuple-element.425, bf16[8192,576]{0,1:T(8,128)(2,1)} %get-tuple-element.424, s32[]{:T(128)S(6)} %select_n.175), kind=kOutput, calls=%fused_computation.2.clone.1 | convolution fusion | flops 605027840 | bytes 3966980 | tf_op jit(solution)/shard_map/while/body/eval_jaxpr/qhc,kc->qhk/dot_general | solution.py:36
  85.9 2.1 %fusion.68 = (bf16[32,16,1024]{2,0,1:T(8,128)(2,1)S(1)}, f32[32,16]{0,1:T(8,128)S(1)}) fusion(f32[1024,32,16]{0,1,2:T(8,128)} %get-tuple-element.386, f32[32,16]{0,1:T(8,128)S(1)} %select_maximum_fusion.2, pred[32,1024]{1,0:T(8,128)(4,1)S(1)} %compare_and_fusion.2), kind=kLoop, calls=%fused_computation.5.clone.1 | loop fusion | flops 2096640 | bytes 3182592 | tf_op jit(solution)/shard_map/while/body/eval_jaxpr/convert_element_type | solution.py:45
  88.2 3.4 %convolution_add_fusion.3 = f32[32,16,512]{2,1,0:T(8,128)} fusion(bf16[8192,576]{0,1:T(8,128)(2,1)} %get-tuple-element.424, s32[]{:T(128)S(6)} %select_n.175, bf16[32,16,1024]{2,0,1:T(8,128)(2,1)S(1)} %get-tuple-element.389, f32[32,16,512]{2,1,0:T(8,128)} %get-tuple-element.407, f32[32,16]{1,0:T(8,128)S(1)} %copy.157, pred[]{:T(512)S(6)} %compare.50), kind=kOutput, calls=%fused_computation.7.clone.1 | convolution fusion | flops 537657344 | bytes 4196357 | tf_op jit(solution)/shard_map/while/body/eval_jaxpr/qhk,kc->qhc/dot_general | solution.py:43
  91.6 0.7 fusion.66
  92.2 0.1 compare_and_fusion.2
  92.3 3.8 %fusion.67 = (f32[32,16]{0,1:T(8,128)S(1)}, f32[1024,32,16]{0,1,2:T(8,128)}) fusion(pred[32,1024]{1,0:T(8,128)(4,1)S(1)} %compare_and_fusion.2, bf16[32,16,576]{2,0,1:T(8,128)(2,1)} %get-tuple-element.425, bf16[8192,576]{0,1:T(8,128)(2,1)} %get-tuple-element.424, s32[]{:T(128)S(6)} %select_n.175), kind=kOutput, calls=%fused_computation.2.clone.1 | convolution fusion | flops 605027840 | bytes 3966980 | tf_op jit(solution)/shard_map/while/body/eval_jaxpr/qhc,kc->qhk/dot_general | solution.py:36
  96.1 2.1 %fusion.68 = (bf16[32,16,1024]{2,0,1:T(8,128)(2,1)S(1)}, f32[32,16]{0,1:T(8,128)S(1)}) fusion(f32[1024,32,16]{0,1,2:T(8,128)} %get-tuple-element.386, f32[32,16]{0,1:T(8,128)S(1)} %select_maximum_fusion.2, pred[32,1024]{1,0:T(8,128)(4,1)S(1)} %compare_and_fusion.2), kind=kLoop, calls=%fused_computation.5.clone.1 | loop fusion | flops 2096640 | bytes 3182592 | tf_op jit(solution)/shard_map/while/body/eval_jaxpr/convert_element_type | solution.py:45
  98.3 3.4 %convolution_add_fusion.3 = f32[32,16,512]{2,1,0:T(8,128)} fusion(bf16[8192,576]{0,1:T(8,128)(2,1)} %get-tuple-element.424, s32[]{:T(128)S(6)} %select_n.175, bf16[32,16,1024]{2,0,1:T(8,128)(2,1)S(1)} %get-tuple-element.389, f32[32,16,512]{2,1,0:T(8,128)} %get-tuple-element.407, f32[32,16]{1,0:T(8,128)S(1)} %copy.157, pred[]{:T(512)S(6)} %compare.50), kind=kOutput, calls=%fused_computation.7.clone.1 | convolution fusion | flops 537657344 | bytes 4196357 | tf_op jit(solution)/shard_map/while/body/eval_jaxpr/qhk,kc->qhc/dot_general | solution.py:43
  101.7 0.7 fusion.66
  102.4 0.1 compare_and_fusion.2
  102.5 3.8 %fusion.67 = (f32[32,16]{0,1:T(8,128)S(1)}, f32[1024,32,16]{0,1,2:T(8,128)}) fusion(pred[32,1024]{1,0:T(8,128)(4,1)S(1)} %compare_and_fusion.2, bf16[32,16,576]{2,0,1:T(8,128)(2,1)} %get-tuple-element.425, bf16[8192,576]{0,1:T(8,128)(2,1)} %get-tuple-element.424, s32[]{:T(128)S(6)} %select_n.175), kind=kOutput, calls=%fused_computation.2.clone.1 | convolution fusion | flops 605027840 | bytes 3966980 | tf_op jit(solution)/shard_map/while/body/eval_jaxpr/qhc,kc->qhk/dot_general | solution.py:36
  106.3 2.1 %fusion.68 = (bf16[32,16,1024]{2,0,1:T(8,128)(2,1)S(1)}, f32[32,16]{0,1:T(8,128)S(1)}) fusion(f32[1024,32,16]{0,1,2:T(8,128)} %get-tuple-element.386, f32[32,16]{0,1:T(8,128)S(1)} %select_maximum_fusion.2, pred[32,1024]{1,0:T(8,128)(4,1)S(1)} %compare_and_fusion.2), kind=kLoop, calls=%fused_computation.5.clone.1 | loop fusion | flops 2096640 | bytes 3182592 | tf_op jit(solution)/shard_map/while/body/eval_jaxpr/convert_element_type | solution.py:45
  108.5 3.4 %convolution_add_fusion.3 = f32[32,16,512]{2,1,0:T(8,128)} fusion(bf16[8192,576]{0,1:T(8,128)(2,1)} %get-tuple-element.424, s32[]{:T(128)S(6)} %select_n.175, bf16[32,16,1024]{2,0,1:T(8,128)(2,1)S(1)} %get-tuple-element.389, f32[32,16,512]{2,1,0:T(8,128)} %get-tuple-element.407, f32[32,16]{1,0:T(8,128)S(1)} %copy.157, pred[]{:T(512)S(6)} %compare.50), kind=kOutput, calls=%fused_computation.7.clone.1 | convolution fusion | flops 537657344 | bytes 4196357 | tf_op jit(solution)/shard_map/while/body/eval_jaxpr/qhk,kc->qhc/dot_general | solution.py:43
  111.9 0.7 fusion.66
  112.6 0.1 compare_and_fusion.2
  112.7 3.8 %fusion.67 = (f32[32,16]{0,1:T(8,128)S(1)}, f32[1024,32,16]{0,1,2:T(8,128)}) fusion(pred[32,1024]{1,0:T(8,128)(4,1)S(1)} %compare_and_fusion.2, bf16[32,16,576]{2,0,1:T(8,128)(2,1)} %get-tuple-element.425, bf16[8192,576]{0,1:T(8,128)(2,1)} %get-tuple-element.424, s32[]{:T(128)S(6)} %select_n.175), kind=kOutput, calls=%fused_computation.2.clone.1 | convolution fusion | flops 605027840 | bytes 3966980 | tf_op jit(solution)/shard_map/while/body/eval_jaxpr/qhc,kc->qhk/dot_general | solution.py:36
  116.5 2.1 %fusion.68 = (bf16[32,16,1024]{2,0,1:T(8,128)(2,1)S(1)}, f32[32,16]{0,1:T(8,128)S(1)}) fusion(f32[1024,32,16]{0,1,2:T(8,128)} %get-tuple-element.386, f32[32,16]{0,1:T(8,128)S(1)} %select_maximum_fusion.2, pred[32,1024]{1,0:T(8,128)(4,1)S(1)} %compare_and_fusion.2), kind=kLoop, calls=%fused_computation.5.clone.1 | loop fusion | flops 2096640 | bytes 3182592 | tf_op jit(solution)/shard_map/while/body/eval_jaxpr/convert_element_type | solution.py:45
  118.7 3.4 %convolution_add_fusion.3 = f32[32,16,512]{2,1,0:T(8,128)} fusion(bf16[8192,576]{0,1:T(8,128)(2,1)} %get-tuple-element.424, s32[]{:T(128)S(6)} %select_n.175, bf16[32,16,1024]{2,0,1:T(8,128)(2,1)S(1)} %get-tuple-element.389, f32[32,16,512]{2,1,0:T(8,128)} %get-tuple-element.407, f32[32,16]{1,0:T(8,128)S(1)} %copy.157, pred[]{:T(512)S(6)} %compare.50), kind=kOutput, calls=%fused_computation.7.clone.1 | convolution fusion | flops 537657344 | bytes 4196357 | tf_op jit(solution)/shard_map/while/body/eval_jaxpr/qhk,kc->qhc/dot_general | solution.py:43
  122.1 0.7 fusion.66
  122.9 3.8 %fusion.67 = (f32[32,16]{0,1:T(8,128)S(1)}, f32[1024,32,16]{0,1,2:T(8,128)}) fusion(pred[32,1024]{1,0:T(8,128)(4,1)S(1)} %compare_and_fusion.2, bf16[32,16,576]{2,0,1:T(8,128)(2,1)} %get-tuple-element.425, bf16[8192,576]{0,1:T(8,128)(2,1)} %get-tuple-element.424, s32[]{:T(128)S(6)} %select_n.175), kind=kOutput, calls=%fused_computation.2.clone.1 | convolution fusion | flops 605027840 | bytes 3966980 | tf_op jit(solution)/shard_map/while/body/eval_jaxpr/qhc,kc->qhk/dot_general | solution.py:36
  126.7 2.1 %fusion.68 = (bf16[32,16,1024]{2,0,1:T(8,128)(2,1)S(1)}, f32[32,16]{0,1:T(8,128)S(1)}) fusion(f32[1024,32,16]{0,1,2:T(8,128)} %get-tuple-element.386, f32[32,16]{0,1:T(8,128)S(1)} %select_maximum_fusion.2, pred[32,1024]{1,0:T(8,128)(4,1)S(1)} %compare_and_fusion.2), kind=kLoop, calls=%fused_computation.5.clone.1 | loop fusion | flops 2096640 | bytes 3182592 | tf_op jit(solution)/shard_map/while/body/eval_jaxpr/convert_element_type | solution.py:45
  128.9 3.4 %convolution_add_fusion.3 = f32[32,16,512]{2,1,0:T(8,128)} fusion(bf16[8192,576]{0,1:T(8,128)(2,1)} %get-tuple-element.424, s32[]{:T(128)S(6)} %select_n.175, bf16[32,16,1024]{2,0,1:T(8,128)(2,1)S(1)} %get-tuple-element.389, f32[32,16,512]{2,1,0:T(8,128)} %get-tuple-element.407, f32[32,16]{1,0:T(8,128)S(1)} %copy.157, pred[]{:T(512)S(6)} %compare.50), kind=kOutput, calls=%fused_computation.7.clone.1 | convolution fusion | flops 537657344 | bytes 4196357 | tf_op jit(solution)/shard_map/while/body/eval_jaxpr/qhk,kc->qhc/dot_general | solution.py:43
  132.6 1.1 multiply_reduce_fusion
  133.7 0.9 fusion.35
  134.6 1.1 multiply_convert_fusion
  135.6 2.1 %select_reduce_fusion = (f32[32,16]{0,1:T(8,128)S(1)}, f32[32,16,64]{2,0,1:T(8,128)}) fusion(pred[32,64]{1,0:T(8,128)(4,1)S(1)} %broadcast_compare_fusion, bf16[32,16,576]{2,0,1:T(8,128)(2,1)} %fusion.17, bf16[64,32]{0,1:T(8,128)(2,1)S(1)} %get-tuple-element.317, bf16[64,32]{0,1:T(8,128)(2,1)S(1)} %get-tuple-element.316, ...), kind=kOutput, calls=%fused_computation.45 | convolution fusion | flops 38034944 | bytes 798720 | tf_op jit(solution)/shard_map/qhc,kc->qhk/dot_general | solution.py:36
  137.9 1.2 fusion.23
  139.2 1.3 convolution_add_fusion.1
  140.6 0.1 constant_dynamic-slice_fusion
  140.7 0.7 copy.107
  141.6 1.8 %all-gather.5 = f32[2,32,16]{1,2,0:T(8,128)S(1)} all-gather(f32[1,32,16]{1,2,0:T(8,128)S(1)} %copy.123), channel_id=4, replica_groups=mesh['groups'=2,'tensor'=8,'seq'=2] {'seq'}, dimensions={0}, use_global_device_ids=true | all-gather | bytes 6144 | tf_op jit(solution)/shard_map/all_gather | solution.py:14
  143.4 1.8 %all-gather.4 = f32[2,32,16]{1,2,0:T(8,128)S(1)} all-gather(f32[1,32,16]{1,2,0:T(8,128)S(1)} %copy.118), channel_id=3, replica_groups=mesh['groups'=2,'tensor'=8,'seq'=2] {'seq'}, dimensions={0}, use_global_device_ids=true | all-gather | bytes 6144 | tf_op jit(solution)/shard_map/all_gather | solution.py:14
  145.5 6.6 %all-gather.8.cloned.1.call-done = f32[64,16,512]{2,1,0:T(8,128)} async-done(((f32[32,16,512]{2,1,0:T(8,128)}), f32[64,16,512]{2,1,0:T(8,128)}) %all-gather.8.cloned.1.call-update) | async-done | bytes 2097168 | tf_op jit(solution)/shard_map/all_gather | solution.py:14
  152.1 2.0 %fusion.20 = f32[32,16,512]{2,1,0:T(8,128)S(1)} fusion(f32[64,16,512]{2,1,0:T(8,128)} %all-gather.8.cloned.1.call-done, f32[32,16]{1,0:T(8,128)S(1)} %copy.124, f32[32,16]{1,0:T(8,128)S(1)} %copy.120, f32[32,16]{1,0:T(8,128)S(1)} %copy.119), kind=kLoop, calls=%fused_computation.40 | loop fusion | flops 1048576 | bytes 3151872 | tf_op jit(solution)/shard_map/div | solution.py:147
  154.1 0.2 copy-done.1
  154.3 1.6 fusion.18
  155.9 0.7 copy.153
  (84 shorter events, 2.1 us)
Async XLA Ops:
  7.2 42.3 %copy-start = (bf16[16,128,512]{2,1,0:T(8,128)(2,1)S(1)}, bf16[16,128,512]{2,1,0:T(8,128)(2,1)}, u32[]{:S(2)}) copy-start(bf16[16,128,512]{2,1,0:T(8,128)(2,1)} %param.19) | copy-start | bytes 6291460
  7.2 125.4 %all-reduce.2.cloned.1.call-start = ((), (), s32[]{:S(2)}) async-start(), calls=%async_computation | async-start | bytes 589824 | tf_op jit(solution)/shard_map/psum | solution.py:135
  9.8 142.3 %all-gather.8.cloned.1.call-start = ((), (), s32[]{:S(2)}) async-start(), calls=%async_computation.1 | async-start | bytes 3145728 | tf_op jit(solution)/shard_map/all_gather | solution.py:14
  48.0 1.1 copy-start.3
  48.0 1.1 copy-start.4
  48.1 1.1 copy-start.5
  132.3 6.9 %copy-start.2 = (f32[32,16,512]{2,1,0:T(8,128)S(1)}, f32[32,16,512]{2,1,0:T(8,128)}, u32[]{:S(2)}) copy-start(f32[32,16,512]{2,1,0:T(8,128)} %get-tuple-element.248) | copy-start | bytes 3145732
  152.1 2.2 %copy-start.1 = (bf16[16,512,128]{2,1,0:T(8,128)(2,1)S(1)}, bf16[16,512,128]{2,1,0:T(8,128)(2,1)}, u32[]{:S(2)}) copy-start(bf16[16,512,128]{2,1,0:T(8,128)(2,1)} %param.20) | copy-start | bytes 6291460
Sparse Core Ops, SparseCore 0:
  11.3 74.1 all-reduce.1
  140.7 11.3 all-gather.7
where the time goes:
time: 165 us; the launch traced here: 163 us
  matrix products  70.4 us (43%)
  blocking collectives  36.3 us (22%)
  other arithmetic  31.2 us (19%)
  between operations  14.9 us (9%)
  waiting for transfers between devices  6.67 us (4%)
  local copies, waits for them, and re-layouts  3.55 us (2%)
    all_gather x1, blocking collectives, body(): latent_piece = lax.all_gather(query_latent, 'tensor', axis=0, tiled=True)  32.7 us
    dot_general x9, matrix products, attend(): jnp.einsum('qhc,kc->qhk', query_full, key_rows, preferred_element_type=jn...  32.3 us
    dot_general x9, matrix products, attend(): jnp.einsum('qhk,kc->qhc', weights.astype(jnp.bfloat16), key_rows[:, :late...  28.2 us
    convert_element_type x9, other arithmetic, attend(): weights.astype(jnp.bfloat16)  18.4 us
    all_gather x1, waiting for transfers between devices, merged(): pieces = jax.tree.map(lambda part: lax.all_gather(part, axis), value)  6.63 us
    dot_general x1, matrix products, body(): jnp.dot(latent_piece, w_up_q, preferred_element_type=jnp.float32)  5.44 us
    not x8, other arithmetic, resident_step(): jnp.logical_not(stale)  5.26 us
    all_gather x2, blocking collectives, merged(): pieces = jax.tree.map(lambda part: lax.all_gather(part, axis), value)  3.63 us
  transfers between devices with their start and end apart: 2, of which 1 were waited for; matrix products, arithmetic and copies ran while one was open for 55% of the time, Pallas kernels for 0%

commit v1 on v0

v1 whole, which is shorter than its diff:
```python
import functools
import numpy as np
import jax
import jax.numpy as jnp
from jax import lax
from jax.experimental import pallas as pl
from jax.experimental.pallas import tpu as pltpu
from jax.sharding import PartitionSpec as P

BLK = 128
NEG = -1e30
FLOOR = -1e20
FAR = 2**30
NORM_EPS = 1e-06
F32 = jnp.float32
BF16 = jnp.bfloat16
MESH = pl.DeviceIdType.MESH


def swap_halves(x):
    half = x.shape[-1] // 2
    return jnp.concatenate([x[:, half:], x[:, :half]], axis=-1)


def trig(pos, freq, rope_dim):
    angle = pos.astype(F32) * freq
    lane = lax.broadcasted_iota(jnp.int32, angle.shape, 1)
    sine = jnp.sin(angle)
    return jnp.cos(angle), jnp.where(lane < rope_dim // 2, -sine, sine)


def kernel(
    cfg,
    eb_ref, qp_ref, pf_ref, freq_ref, gain_ref,
    hid_hbm, wd_hbm, ql_hbm, wq_hbm, wk_hbm, wv_hbm, kc_hbm,
    reb_ref, att_ref,
    hid, wd, ql, qlf, wq, wk, wv, kc,
    qf, part, rsum, rown, rall, m_s, l_s, acc_s, lim_s, osend, orecv,
    w_sem, q_sem, c_sem, ql_ss, ql_rs, rs_ss, rs_rs, ag_ss, ag_rs, ex_ss, ex_rs,
):
    T, heads, nope, rank, rope_dim, Q, requests, nq, nb, bk, ng = cfg
    me = lax.axis_index("tensor")
    sq = lax.axis_index("seq")
    other = 1 - sq
    head_qk = nope + rope_dim
    piece = ql_hbm.shape[0]
    half_rows = hid.shape[0]
    local = half_rows // T
    R = heads * Q
    n_evicted = eb_ref.shape[0]
    hq = heads // nq

    def far(d):
        return lax.rem(me + d, T)

    def near(d):
        return lax.rem(me + T - d, T)

    barrier = pltpu.get_barrier_semaphore()
    for d in range(1, T):
        pl.semaphore_signal(barrier, inc=1, device_id={"tensor": far(d)}, device_id_type=MESH)
    pl.semaphore_signal(barrier, inc=1, device_id={"seq": other}, device_id_type=MESH)

    own_q = pltpu.make_async_copy(ql_hbm, ql.at[me], w_sem.at[0])
    c_hid = pltpu.make_async_copy(hid_hbm.at[0], hid, w_sem.at[1])
    c_wd = pltpu.make_async_copy(wd_hbm, wd, w_sem.at[2])
    c_wk = pltpu.make_async_copy(wk_hbm, wk, w_sem.at[3])
    c_wv = pltpu.make_async_copy(wv_hbm, wv, w_sem.at[4])
    wide = hq * head_qk
    c_wq = [
        pltpu.make_async_copy(
            wq_hbm.at[:, pl.ds(i * wide, wide)], wq.at[:, pl.ds(i * wide, wide)], q_sem.at[i]
        )
        for i in range(nq)
    ]

    def c_kc(i):
        cols = pl.ds(pl.multiple_of(i * bk, bk), bk)
        return pltpu.make_async_copy(kc_hbm.at[:, cols], kc.at[i], c_sem.at[i])

    own_q.start()
    c_hid.start()
    c_wd.start()
    for c in c_wq:
        c.start()
    c_wk.start()
    for i in range(nb):
        c_kc(i).start()
    c_wv.start()

    freq = freq_ref[...]
    qrow = lax.broadcasted_iota(jnp.int32, (Q, 1), 0)
    qpos = lax.fori_loop(
        0, Q, lambda i, v: jnp.where(qrow == i, qp_ref[i], v), jnp.zeros((Q, 1), jnp.int32)
    )
    qcos, qsin = trig(qpos, freq, rope_dim)
    per = Q // requests
    limit = jnp.zeros((Q, 1), jnp.int32)
    for r in range(requests):
        limit = jnp.where((qrow >= r * per) & (qrow < (r + 1) * per), pf_ref[r], limit)
    for h in range(heads):
        lim_s[h * Q:(h + 1) * Q, :] = limit
    m_s[...] = jnp.full(m_s.shape, FLOOR, F32)
    l_s[...] = jnp.zeros(l_s.shape, F32)
    acc_s[...] = jnp.zeros(acc_s.shape, F32)
    flat0 = sq * half_rows + me * local
    rpos = (
        eb_ref[flat0 // BLK] * BLK + flat0 % BLK
        + lax.broadcasted_iota(jnp.int32, (local, 1), 0)
    )
    rcos, rsin = trig(rpos, freq, rope_dim)

    pl.semaphore_wait(barrier, T)

    def ql_copy(d, slot):
        return pltpu.make_async_remote_copy(
            src_ref=ql_hbm, dst_ref=ql.at[slot], send_sem=ql_ss.at[d], recv_sem=ql_rs.at[d],
            device_id={"tensor": far(d)}, device_id_type=MESH,
        )

    def rs_copy(d, slot):
        return pltpu.make_async_remote_copy(
            src_ref=part.at[far(d)], dst_ref=rsum.at[slot], send_sem=rs_ss.at[d],
            recv_sem=rs_rs.at[d], device_id={"tensor": far(d)}, device_id_type=MESH,
        )

    def ag_copy(d, slot):
        return pltpu.make_async_remote_copy(
            src_ref=rown, dst_ref=rall.at[slot], send_sem=ag_ss.at[d], recv_sem=ag_rs.at[d],
            device_id={"tensor": far(d)}, device_id_type=MESH,
        )

    for d in range(1, T):
        ql_copy(d, me).start()

    c_hid.wait()
    c_wd.wait()
    partial = lax.dot_general(
        hid[...], wd[...], (((1,), (1,)), ((), ())), preferred_element_type=F32
    )
    for t in range(T):
        part[t] = partial[t * local:(t + 1) * local, :]
    rsum[me] = part[me]
    for d in range(1, T):
        rs_copy(d, me).start()

    own_q.wait()
    for d in range(1, T):
        ql_copy(d, near(d)).wait_recv()
    for t in range(T):
        qlf[t * piece:(t + 1) * piece, :] = ql[t].astype(F32)
    queries = qlf[...].astype(BF16)
    scale = float(head_qk) ** (-0.5)
    for i in range(nq):
        c_wq[i].wait()
        if i == 0:
            c_wk.wait()
        proj = jnp.dot(
            queries, wq[:, i * wide:(i + 1) * wide], preferred_element_type=F32
        )
        for j in range(hq):
            h = i * hq + j
            q_nope = proj[:, j * head_qk:j * head_qk + nope].astype(BF16)
            q_rope = proj[:, j * head_qk + nope:(j + 1) * head_qk]
            absorbed = jnp.dot(q_nope, wk[h], preferred_element_type=F32)
            qf[h * Q:(h + 1) * Q, :rank] = (absorbed * scale).astype(BF16)
            turned = q_rope * qcos + swap_halves(q_rope) * qsin
            qf[h * Q:(h + 1) * Q, rank:] = (turned * scale).astype(BF16)

    for d in range(1, T):
        rs_copy(d, near(d)).wait_recv()
    summed = rsum[0]
    for t in range(1, T):
        summed = summed + rsum[t]
    latent = summed[:, :rank]
    mean_square = jnp.mean(latent * latent, axis=-1, keepdims=True)
    normed = latent / jnp.sqrt(mean_square + NORM_EPS) * gain_ref[...].astype(F32).reshape(1, rank)
    tail = summed[:, rank:]
    turned = tail * rcos + swap_halves(tail) * rsin
    rown[:, :rank] = normed.astype(BF16)
    rown[:, rank:] = turned.astype(BF16)
    reb_ref[0] = rown[...]
    rall[me] = rown[...]
    for d in range(1, T):
        ag_copy(d, me).start()

    halves = 2
    rr = R // halves

    def attend(keys, pos, key_dim):
        values = keys[:rank, :] if key_dim else keys[:, :rank]
        for g in range(halves):
            rows = pl.ds(g * rr, rr)
            s = lax.dot_general(
                qf[rows, :], keys, (((1,), (1 - key_dim,)), ((), ())), preferred_element_type=F32
            )
            s = jnp.where(pos < lim_s[rows, :], s, NEG)
            m_old = m_s[rows, :]
            m_new = jnp.maximum(m_old, jnp.max(s, axis=1, keepdims=True))
            p = jnp.exp(s - m_new)
            alpha = jnp.exp(m_old - m_new)
            m_s[rows, :] = m_new
            l_s[rows, :] = l_s[rows, :] * alpha + jnp.sum(p, axis=1, keepdims=True)
            acc_s[rows, :] = acc_s[rows, :] * alpha + lax.dot_general(
                p.astype(BF16), values, (((1,), (key_dim,)), ((), ())),
                preferred_element_type=F32,
            )

    def step(i, carry):
        c_kc(i).wait()
        pos = sq * (nb * bk) + i * bk + lax.broadcasted_iota(jnp.int32, (1, bk), 1)
        eff = pos
        for e in range(n_evicted):
            first = eb_ref[e] * BLK
            eff = jnp.where((pos >= first) & (pos < first + BLK), FAR, eff)
        attend(kc[i], eff, 1)
        return carry

    lax.fori_loop(0, nb, step, 0)

    for d in range(1, T):
        ag_copy(d, near(d)).wait_recv()
    fresh = jnp.concatenate([rall[t].astype(F32) for t in range(T)], axis=0).astype(BF16)
    flat = sq * half_rows + lax.broadcasted_iota(jnp.int32, (1, half_rows), 1)
    fpos = flat
    for e in range(n_evicted):
        inside = (flat >= e * BLK) & (flat < (e + 1) * BLK)
        fpos = jnp.where(inside, eb_ref[e] * BLK + flat - e * BLK, fpos)
    attend(fresh, fpos, 0)

    vh = wv.shape[2]
    gcols = (heads // ng) * vh

    def ex_copy(g):
        cols = pl.ds(g * gcols, gcols) if g < ng else pl.ds(heads * vh, 128)
        return pltpu.make_async_remote_copy(
            src_ref=osend.at[:, cols], dst_ref=orecv.at[:, cols], send_sem=ex_ss.at[g],
            recv_sem=ex_rs.at[g], device_id={"seq": other}, device_id_type=MESH,
        )

    lane = lax.broadcasted_iota(jnp.int32, (Q, 128), 1)
    stats = jnp.zeros((Q, 128), F32)
    for h in range(heads):
        stats = jnp.where(lane == h, m_s[h * Q:(h + 1) * Q, :], stats)
        stats = jnp.where(lane == heads + h, l_s[h * Q:(h + 1) * Q, :], stats)
    osend[:, heads * vh:] = stats
    ex_copy(ng).start()
    c_wv.wait()
    for g in range(ng):
        for h in range(g * (heads // ng), (g + 1) * (heads // ng)):
            a = acc_s[h * Q:(h + 1) * Q, :]
            high = a.astype(BF16)
            low = (a - high.astype(F32)).astype(BF16)
            both = jnp.dot(
                jnp.concatenate([high, low], axis=0), wv[h], preferred_element_type=F32
            )
            osend[:, h * vh:(h + 1) * vh] = both[:Q] + both[Q:]
        ex_copy(g).start()

    ex_copy(ng).wait_recv()
    theirs = orecv[:, heads * vh:]
    m_a, m_b = stats[:, :heads], theirs[:, :heads]
    joint = jnp.maximum(m_a, m_b)
    e_a, e_b = jnp.exp(m_a - joint), jnp.exp(m_b - joint)
    total = e_a * stats[:, heads:2 * heads] + e_b * theirs[:, heads:2 * heads]
    e_a, e_b = e_a / total, e_b / total
    for g in range(ng):
        ex_copy(g).wait_recv()
        for h in range(g * (heads // ng), (g + 1) * (heads // ng)):
            cols = slice(h * vh, (h + 1) * vh)
            att_ref[:, cols] = (
                e_a[:, h:h + 1] * osend[:, cols] + e_b[:, h:h + 1] * orecv[:, cols]
            ).astype(BF16)

    for d in range(1, T):
        ql_copy(d, me).wait_send()
        rs_copy(d, me).wait_send()
        ag_copy(d, me).wait_send()
    for g in range(ng + 1):
        ex_copy(g).wait_send()


def body(
    stored_hidden, w_down_kv, kv_gain, evicted_blocks, query_latent, w_up_q,
    w_key_absorb, w_value, query_positions, prefix_lengths, latent_cache,
):
    T = lax.axis_size("tensor")
    rank = kv_gain.shape[0]
    heads, nope = w_key_absorb.shape[:2]
    width = w_down_kv.shape[1]
    rope_dim = width - rank
    Q = query_positions.shape[0]
    requests = prefix_lengths.shape[0]
    half_rows = stored_hidden.shape[1]
    local = half_rows // T
    cache_rows = latent_cache.shape[0]
    bk = min(1024, cache_rows)
    nb = cache_rows // bk
    nq = max(1, heads // 4)
    ng = max(1, heads // 4)
    vh = w_value.shape[2]
    R = heads * Q
    half = np.arange(rope_dim // 2, dtype=np.float64) * (-2.0 / rope_dim)
    freq = jnp.asarray(np.tile(10000.0 ** half, 2)[None, :].astype(np.float32))
    cfg = (T, heads, nope, rank, rope_dim, Q, requests, nq, nb, bk, ng)
    smem = pl.BlockSpec(memory_space=pltpu.SMEM)
    vmem = pl.BlockSpec(memory_space=pltpu.VMEM)
    hbm = pl.BlockSpec(memory_space=pl.ANY)
    dma = pltpu.SemaphoreType.DMA
    return pl.pallas_call(
        functools.partial(kernel, cfg),
        name="rebuild_attend",
        out_shape=(
            jax.ShapeDtypeStruct((1, local, width), BF16),
            jax.ShapeDtypeStruct((Q, heads * vh), BF16),
        ),
        in_specs=[smem] * 3 + [vmem] * 2 + [hbm] * 7,
        out_specs=(vmem, vmem),
        scratch_shapes=[
            pltpu.VMEM((half_rows, w_down_kv.shape[0]), BF16),
            pltpu.VMEM(w_down_kv.shape[::-1], BF16),
            pltpu.VMEM((T,) + query_latent.shape, BF16),
            pltpu.VMEM((Q, query_latent.shape[1]), F32),
            pltpu.VMEM(w_up_q.shape, BF16),
            pltpu.VMEM(w_key_absorb.shape, BF16),
            pltpu.VMEM(w_value.shape, BF16),
            pltpu.VMEM((nb, width, bk), BF16),
            pltpu.VMEM((R, width), BF16),
            pltpu.VMEM((T, local, width), F32),
            pltpu.VMEM((T, local, width), F32),
            pltpu.VMEM((local, width), BF16),
            pltpu.VMEM((T, local, width), BF16),
            pltpu.VMEM((R, 1), F32),
            pltpu.VMEM((R, 1), F32),
            pltpu.VMEM((R, rank), F32),
            pltpu.VMEM((R, 1), jnp.int32),
            pltpu.VMEM((Q, heads * vh + 128), F32),
            pltpu.VMEM((Q, heads * vh + 128), F32),
            dma((5,)), dma((nq,)), dma((nb,)),
            dma((T,)), dma((T,)), dma((T,)), dma((T,)), dma((T,)), dma((T,)),
            dma((ng + 1,)), dma((ng + 1,)),
        ],
        compiler_params=pltpu.CompilerParams(
            collective_id=0, has_side_effects=True, vmem_limit_bytes=60 * 1024 * 1024
        ),
    )(
        evicted_blocks, query_positions, prefix_lengths, freq, kv_gain,
        stored_hidden, w_down_kv.T, query_latent, w_up_q, w_key_absorb, w_value, latent_cache.T,
    )


def solution(mesh):
    placed = (
        P(("groups", "seq"), None, "tensor"),
        P("tensor", None),
        P(),
        P("groups"),
        P(("groups", "tensor"), None),
        P(None, "tensor"),
        P("tensor", None, None),
        P("tensor", None, None),
        P("groups"),
        P("groups"),
        P(("groups", "seq"), None),
    )
    return jax.shard_map(
        body,
        mesh=mesh,
        in_specs=placed,
        out_specs=(P(("groups", "seq"), "tensor", None), P("groups", "tensor")),
        check_vma=False,
    )
```

time: 165 us -> 40.1 us (0.24)
  matrix products: 70.4 us -> 0 us
  blocking collectives: 36.3 us -> 0 us
  Pallas kernels: 0 us -> 35.6 us
  other arithmetic: 31.2 us -> 0 us
  between operations: 14.9 us -> 1.29 us
  waiting for transfers between devices: 6.67 us -> 0 us
    dot_general x22 -> x0, matrix products: 70.4 us -> none  [the longest x9 32.3 us: attend(): jnp.einsum('qhc,kc->qhk', query_full, key_rows, preferred_element_type=jn...]
    all_gather x3 -> x0, blocking collectives: 36.3 us -> none  [the longest x1 32.7 us: body(): latent_piece = lax.all_gather(query_latent, 'tensor', axis=0, tiled=True)]
    pallas_call x0 -> x1, Pallas kernels: none -> 35.6 us  [body(): pl.pallas_call(functools.partial(kernel, cfg), name='rebuild_attend', out...]
    convert_element_type x13 -> x0, other arithmetic: 19.5 us -> none  [the longest x9 18.4 us: attend(): weights.astype(jnp.bfloat16)]
    all_gather x1 -> x0, waiting for transfers between devices: 6.63 us -> none  [merged(): pieces = jax.tree.map(lambda part: lax.all_gather(part, axis), value)]
    not x8 -> x0, other arithmetic: 5.26 us -> none  [resident_step(): jnp.logical_not(stale)]
    unnamed x17 -> x2, local copies, waits for them, and re-layouts: 0.59 us -> 2.87 us
    div x1 -> x0, other arithmetic: 1.96 us -> none  [body(): latent_out = whole_acc / whole_sum[..., None]]
  transfers between devices with their start and end apart: 2 -> 0, of which waited for: 1 -> 0; matrix products, arithmetic and copies ran while one was open for 55% -> 0% of each run, Pallas kernels for 0% -> 0%
where the time goes in v1:
time: 40.1 us; the launch traced here: 39.7 us
  Pallas kernels  35.6 us (89%)
  local copies, waits for them, and re-layouts  2.87 us (7%)
  between operations  1.29 us (3%)
    pallas_call x1, Pallas kernels, body(): pl.pallas_call(functools.partial(kernel, cfg), name='rebuild_attend', out...  35.6 us
    unnamed x2, local copies, waits for them, and re-layouts  2.87 us

profile of v1, /device:TPU:0, one launch (start us, length us, event | category | flops | bytes accessed | tf_op | source)
XLA Modules:
  0.0 39.7 jit_solution(15881527279342012183)
XLA Ops:
  1.3 35.6 %rebuild_attend.1 = (bf16[1,8,576]{2,1,0:T(8,128)(2,1)}, bf16[32,2048]{1,0:T(8,128)(2,1)}) custom-call(s32[1]{0:T(128)S(6)} %copy.16.eb_ref, s32[32]{0:T(128)} %qp_ref.1, s32[4]{0:T(128)} %pf_ref.1, f32[1,64]{1,0:T(1,128)} %constant.2.clone.freq_ref, bf16[512]{0:T(512)(128)(2,1)} %gain_ref.1, bf16[1,64,896]{2,1,0:T(8,128)(2,1)} %hid_hbm.1, ...), custom_call_target="tpu_custom_call" | custom-call | tf_op jit(solution)/shard_map/rebuild_attend/pallas_call | solution.py:310
  36.8 1.3 %copy.17 = bf16[1,8,576]{2,1,0:T(8,128)(2,1)} copy(bf16[1,8,576]{2,1,0:T(8,128)(2,1)} %get-tuple-element.4) | data formatting | bytes 18432
  38.1 1.6 %copy.18 = bf16[32,2048]{1,0:T(8,128)(2,1)} copy(bf16[32,2048]{1,0:T(8,128)(2,1)} %get-tuple-element.5) | data formatting | bytes 262144

commit v2 on v1

--- a/solution.py
+++ b/solution.py
@@ -167,23 +167,6 @@
             turned = q_rope * qcos + swap_halves(q_rope) * qsin
             qf[h * Q:(h + 1) * Q, rank:] = (turned * scale).astype(BF16)
 
-    for d in range(1, T):
-        rs_copy(d, near(d)).wait_recv()
-    summed = rsum[0]
-    for t in range(1, T):
-        summed = summed + rsum[t]
-    latent = summed[:, :rank]
-    mean_square = jnp.mean(latent * latent, axis=-1, keepdims=True)
-    normed = latent / jnp.sqrt(mean_square + NORM_EPS) * gain_ref[...].astype(F32).reshape(1, rank)
-    tail = summed[:, rank:]
-    turned = tail * rcos + swap_halves(tail) * rsin
-    rown[:, :rank] = normed.astype(BF16)
-    rown[:, rank:] = turned.astype(BF16)
-    reb_ref[0] = rown[...]
-    rall[me] = rown[...]
-    for d in range(1, T):
-        ag_copy(d, me).start()
-
     halves = 2
     rr = R // halves
 
@@ -216,7 +199,27 @@
         attend(kc[i], eff, 1)
         return carry
 
-    lax.fori_loop(0, nb, step, 0)
+    early = max(1, nb // 2)
+    lax.fori_loop(0, early, step, 0)
+
+    for d in range(1, T):
+        rs_copy(d, near(d)).wait_recv()
+    summed = rsum[0]
+    for t in range(1, T):
+        summed = summed + rsum[t]
+    latent = summed[:, :rank]
+    mean_square = jnp.mean(latent * latent, axis=-1, keepdims=True)
+    normed = latent / jnp.sqrt(mean_square + NORM_EPS) * gain_ref[...].astype(F32).reshape(1, rank)
+    tail = summed[:, rank:]
+    turned = tail * rcos + swap_halves(tail) * rsin
+    rown[:, :rank] = normed.astype(BF16)
+    rown[:, rank:] = turned.astype(BF16)
+    reb_ref[0] = rown[...]
+    rall[me] = rown[...]
+    for d in range(1, T):
+        ag_copy(d, me).start()
+
+    lax.fori_loop(early, nb, step, 0)
 
     for d in range(1, T):
         ag_copy(d, near(d)).wait_recv()
@@ -280,6 +283,11 @@
         ex_copy(g).wait_send()
 
 
+def hand_over(reb_in, att_in, reb_out, att_out):
+    reb_out[...] = reb_in[...]
+    att_out[...] = att_in[...]
+
+
 def body(
     stored_hidden, w_down_kv, kv_gain, evicted_blocks, query_latent, w_up_q,
     w_key_absorb, w_value, query_positions, prefix_lengths, latent_cache,
@@ -294,7 +302,7 @@
     half_rows = stored_hidden.shape[1]
     local = half_rows // T
     cache_rows = latent_cache.shape[0]
-    bk = min(1024, cache_rows)
+    bk = min(2048, cache_rows)
     nb = cache_rows // bk
     nq = max(1, heads // 4)
     ng = max(1, heads // 4)
@@ -307,7 +315,7 @@
     vmem = pl.BlockSpec(memory_space=pltpu.VMEM)
     hbm = pl.BlockSpec(memory_space=pl.ANY)
     dma = pltpu.SemaphoreType.DMA
-    return pl.pallas_call(
+    outs = pl.pallas_call(
         functools.partial(kernel, cfg),
         name="rebuild_attend",
         out_shape=(
@@ -347,6 +355,13 @@
         evicted_blocks, query_positions, prefix_lengths, freq, kv_gain,
         stored_hidden, w_down_kv.T, query_latent, w_up_q, w_key_absorb, w_value, latent_cache.T,
     )
+    return pl.pallas_call(
+        hand_over,
+        name="hand_over",
+        out_shape=tuple(jax.ShapeDtypeStruct(o.shape, o.dtype) for o in outs),
+        in_specs=[vmem] * 2,
+        out_specs=(vmem, vmem),
+    )(*outs)
 
 
 def solution(mesh):

time: 40.1 us -> 37.3 us (0.930)
  local copies, waits for them, and re-layouts: 2.87 us -> 0 us
    unnamed x2 -> x0, local copies, waits for them, and re-layouts: 2.87 us -> none
    pallas_call x0 -> x1, Pallas kernels: none -> 1.59 us  [body(): pl.pallas_call(hand_over, name='hand_over', out_shape=tuple((jax.ShapeDty...]
    pallas_call x1, Pallas kernels: 35.6 us -> 34.2 us  [body(): pl.pallas_call(functools.partial(kernel, cfg), name='rebuild_attend', out...]
where the time goes in v2:
time: 37.3 us; the launch traced here: 37.1 us
  Pallas kernels  35.8 us (96%)
  between operations  1.29 us (3%)
    pallas_call x1, Pallas kernels, body(): pl.pallas_call(functools.partial(kernel, cfg), name='rebuild_attend', out...  34.2 us
    pallas_call x1, Pallas kernels, body(): pl.pallas_call(hand_over, name='hand_over', out_shape=tuple((jax.ShapeDty...  1.59 us

profile of v2, /device:TPU:0, one launch (start us, length us, event | category | flops | bytes accessed | tf_op | source)
XLA Modules:
  0.0 37.1 jit_solution(10082140665151781206)
XLA Ops:
  1.3 34.2 %rebuild_attend.1 = (bf16[1,8,576]{2,1,0:T(8,128)(2,1)}, bf16[32,2048]{1,0:T(8,128)(2,1)}) custom-call(s32[1]{0:T(128)S(6)} %copy.14.eb_ref, s32[32]{0:T(128)} %qp_ref.1, s32[4]{0:T(128)} %pf_ref.1, f32[1,64]{1,0:T(1,128)} %constant.2.clone.freq_ref, bf16[512]{0:T(512)(128)(2,1)} %gain_ref.1, bf16[1,64,896]{2,1,0:T(8,128)(2,1)} %hid_hbm.1, ...), custom_call_target="tpu_custom_call" | custom-call | tf_op jit(solution)/shard_map/rebuild_attend/pallas_call | solution.py:318
  35.5 1.6 %hand_over.1 = (bf16[1,8,576]{2,1,0:T(8,128)(2,1)}, bf16[32,2048]{1,0:T(8,128)(2,1)}) custom-call(bf16[1,8,576]{2,1,0:T(8,128)(2,1)} %get-tuple-element.4.reb_in, bf16[32,2048]{1,0:T(8,128)(2,1)} %get-tuple-element.5.att_in), custom_call_target="tpu_custom_call" | custom-call | tf_op jit(solution)/shard_map/hand_over/pallas_call | solution.py:358
